TPU v7x, 32 devices: a whole 2x2x4 slice. The times are simulated.
32 devices in a mesh: groups: 2 (over y), tile: 4 (over z), sub: 2 (over x), rep: 2 (over core).
Axes of the slice: x: 2, y: 2, z: 4, core: 2. Of those that a mesh axis runs over, the one named last changes fastest.
Arguments:
- pressure: float32 [64, 32, 256], P(('groups', 'tile'), 'sub', 'rep'), parts along dimension 0, may hold values from -3 to 3
- previous_pressure: float32 [64, 32, 256], P(('groups', 'tile'), 'sub', 'rep'), parts along dimension 0, may hold values from -3 to 3
- courant_square: float32 [64, 32, 256], P(('groups', 'tile'), 'sub', 'rep'), parts along dimension 0, may hold values from 0.07 to 0.22
- node_area: float32 [12288], P(('groups', 'tile', 'sub', 'rep')), parts along dimension 0, may hold values from 0.25 to 4
- mode_shapes: bfloat16 [12288, 2048], P(('groups', 'tile', 'sub', 'rep')), parts along dimension 0, may hold values from -0.049804688 to 0.049804688
- frequency: float32 [4096], P('groups'), parts along dimension 0, may hold values from 0.4 to 1.3
- damping_ratio: float32 [4096], P('groups'), parts along dimension 0, may hold values from 0.02 to 0.4
- modal_start: float32 [2, 4096], P(None, 'groups'), parts along dimension 1, may hold values from -4 to 4
- slot_cell: int32 [8, 2, 2, 384], P(('groups', 'tile'), 'sub', 'rep'), parts along dimension 0, may hold values from 0 to 16383, as said below
- slot_owner: int32 [8, 2, 2, 384, 1], P(('groups', 'tile'), 'sub', 'rep'), parts along dimension 0, may hold values from 0 to 3; in each aligned block of 384 rows (0 to 383, 384 to 767, ..., all dimensions but the last counted through in order) at most 96 rows name the same one
- surface_count: int32 [4, 2, 4], P(('groups', 'sub'), 'rep', 'tile'), parts along dimension 0, may hold values from 1 to 384, 512 in all within a row
Outputs:
- final_pressure: float32 [64, 32, 256], P(('groups', 'tile'), 'sub', 'rep'), parts along dimension 0
- prior_pressure: float32 [64, 32, 256], P(('groups', 'tile'), 'sub', 'rep'), parts along dimension 0
- surface_accel: bfloat16 [8, 2, 2, 4, 384], P(('groups', 'tile'), 'sub', 'rep'), parts along dimension 0
- modal_state: float32 [2, 4096], P(None, ('groups', 'tile', 'sub', 'rep')), parts along dimension 1
There are 2 independent parts, one for each index of `groups`. A program takes and returns all parts, laid end to end along the dimension named above; each array names one. Nothing has to cross between parts.
Inputs may be any that keep to these rules, and one draw needn't show every extreme that they name: `slot_cell`: slot j of a block lies in the block's cells j * (42) to (j + 1) (42) - 1, so a block's slots name distinct cells. `slot_owner`: every owner index is named by exactly 96 of the 384 slots of each block (t, s, r). `surface_count`: for fixed s and r the counts over t sum to 128 times the number of tile indices, and one of them equals 384.
All inputs are finite; a program needn't handle non-finite values. No bound on the sum of `surface_count` on one device may be relied on, other than what follows from the above.
Results may differ from a plain program's by a relative error of at most 0.0098.
Values may be sent and summed in bfloat16 or wider, within the bound.
A program may use at most 64 MiB of HBM per device.

v0:
```python
import jax
import jax.numpy as jnp
from jax import lax
from jax.sharding import PartitionSpec as P

STEPS = 4
HALO = 4


nonlinear = 0.03
viscous = 0.02


def extended(shard, sides, width):
    for axis, dim in sides:
        count, length = (lax.axis_size(axis), shard.shape[dim])
        up = [(i, (i + 1) % count) for i in range(count - 1)]
        down = [(j, i) for i, j in up]
        last = lax.slice_in_dim(shard, length - width, length, axis=dim)
        first = lax.slice_in_dim(shard, 0, width, axis=dim)
        before = lax.ppermute(last, axis, up)
        after = lax.ppermute(first, axis, down)
        shard = jnp.concatenate([before, shard, after], axis=dim)
    return shard


def laplace(padded):
    middle = padded[1:-1, 1:-1, 1:-1]
    summed = padded[2:, 1:-1, 1:-1] + padded[:-2, 1:-1, 1:-1]
    summed = summed + padded[1:-1, 2:, 1:-1] + padded[1:-1, :-2, 1:-1]
    summed = summed + padded[1:-1, 1:-1, 2:] + padded[1:-1, 1:-1, :-2]
    return summed - 6.0 * middle


def advance(wide_now, wide_before, coefficient):
    current = wide_now[1:-1, 1:-1, 1:-1]
    before = wide_before[1:-1, 1:-1, 1:-1]
    change = current - before
    driving = (
        coefficient * laplace(wide_now)
        + viscous * laplace(wide_now - wide_before)
        + 2.0 * nonlinear * change * change
    )
    return 2.0 * current - before + (1.0 + 2.0 * nonlinear * current) * driving


def routing(owners, live_count, tile_total):
    slot_total = owners.shape[0]
    bucket = slot_total // tile_total
    position = jnp.arange(slot_total, dtype=jnp.int32)
    is_live = position < live_count
    member = (
        (owners[:, None] == jnp.arange(tile_total, dtype=jnp.int32)[None, :]) & is_live[:, None]
    ).astype(jnp.float32)
    earlier = (position[None, :] < position[:, None]).astype(jnp.float32)
    before = jnp.dot(earlier, member, precision=lax.Precision.HIGHEST)
    bucket_rank = jnp.sum(before * member, axis=1).astype(jnp.int32)
    target = owners * bucket + bucket_rank
    return ((target[:, None] == position[None, :]) & is_live[:, None]).astype(jnp.bfloat16)


def oscillate(forces, frequency, damping_ratio, start_state):

    def advance_mode(carried, force_row):
        displace, velocity = carried
        acceleration = (
            force_row
            - 2.0 * damping_ratio * frequency * velocity
            - frequency * frequency * displace
        )
        velocity = velocity + acceleration
        displace = displace + velocity
        return ((displace, velocity), acceleration)

    (displace, velocity), modal_accel = lax.scan(
        advance_mode, (start_state[0], start_state[1]), forces
    )
    return (modal_accel, jnp.stack([displace, velocity]))


def trim_rim(array, depth):
    return array[
        depth : array.shape[0] - depth,
        depth : array.shape[1] - depth,
        depth : array.shape[2] - depth,
    ]


def inside_range(offset, length, axis_devices, margin):
    position = offset * length - margin + jnp.arange(length + 2 * margin, dtype=jnp.int32)
    return ((position >= 0) & (position < axis_devices * length)).astype(jnp.float32)


def body(
    pressure,
    previous_pressure,
    courant_square,
    node_area,
    mode_shapes,
    frequency,
    damping_ratio,
    modal_start,
    slot_cell,
    slot_owner,
    surface_count,
):
    tile_total = lax.axis_size("tile")
    extent_first, extent_second, extent_third = pressure.shape
    slot_total = slot_cell.shape[-1]
    bucket = slot_total // tile_total
    routing_matrix = routing(slot_owner.reshape(slot_total), surface_count.reshape(()), tile_total)
    cell_index = slot_cell.reshape(slot_total)
    fields = jnp.stack([pressure, previous_pressure])
    margin = HALO
    coef_wide = extended(courant_square, (("tile", 0), ("sub", 1), ("rep", 2)), margin)
    inside_first = inside_range(lax.axis_index("tile"), extent_first, lax.axis_size("tile"), margin)
    inside_second = inside_range(lax.axis_index("sub"), extent_second, lax.axis_size("sub"), margin)
    inside_third = inside_range(lax.axis_index("rep"), extent_third, lax.axis_size("rep"), margin)
    inside = (
        inside_first[:, None, None] * inside_second[None, :, None] * inside_third[None, None, :]
    )

    def deep_block(carried, unused):
        padded = extended(carried, (("tile", 1), ("sub", 2), ("rep", 3)), margin)
        recorded = []
        for layer_index in range(margin):
            edge_depth = layer_index + 1
            updated = advance(padded[0], padded[1], trim_rim(coef_wide, edge_depth)) * trim_rim(
                inside, edge_depth
            )
            interior = trim_rim(updated, margin - edge_depth)
            recorded.append(jnp.take(interior.reshape(-1), cell_index).astype(jnp.bfloat16))
            padded = jnp.stack([updated, trim_rim(padded[0], 1)])
        return (padded, jnp.stack(recorded))

    fields, history = lax.scan(deep_block, fields, None, length=STEPS // margin)
    history = history.reshape(STEPS, slot_total)
    final_field = fields[0]
    prior_field = fields[1]
    bucketed = jnp.dot(history, routing_matrix, preferred_element_type=jnp.float32).astype(
        jnp.bfloat16
    )
    bucketed = bucketed.reshape(STEPS, tile_total, bucket)
    arrived = lax.all_to_all(bucketed, "tile", split_axis=1, concat_axis=1, tiled=True)
    arrived_flat = arrived.reshape(arrived.shape[0], slot_total)
    weighted = (arrived_flat * node_area).astype(jnp.bfloat16)
    partial_forces = jnp.dot(weighted, mode_shapes, preferred_element_type=jnp.float32)
    device_total = lax.axis_size("tile") * lax.axis_size("sub") * lax.axis_size("rep")
    mode_count = mode_shapes.shape[1]
    mode_share = mode_count // device_total
    first_mode = lax.axis_index(("tile", "sub", "rep")) * mode_share
    forces = lax.psum_scatter(
        partial_forces, ("tile", "sub", "rep"), scatter_dimension=1, tiled=True
    )
    local_frequency = lax.dynamic_slice_in_dim(frequency, first_mode, mode_share, 0)
    local_damping = lax.dynamic_slice_in_dim(damping_ratio, first_mode, mode_share, 0)
    local_start = lax.dynamic_slice_in_dim(modal_start, first_mode, mode_share, 1)
    modal_accel, modal_state = oscillate(forces, local_frequency, local_damping, local_start)
    modal_rounded = modal_accel.astype(jnp.bfloat16)
    node_accel = lax.dot_general(
        lax.all_gather(modal_rounded, ("tile", "sub", "rep"), axis=1, tiled=True),
        mode_shapes,
        (((1,), (1,)), ((), ())),
        preferred_element_type=jnp.float32,
    )
    outgoing = node_accel.astype(jnp.bfloat16).reshape(STEPS, tile_total, bucket)
    returned = lax.all_to_all(outgoing, "tile", split_axis=1, concat_axis=1, tiled=True)
    surface = lax.dot_general(
        returned.reshape(STEPS, slot_total),
        routing_matrix,
        (((1,), (1,)), ((), ())),
        preferred_element_type=jnp.float32,
    )
    surface_accel = surface.astype(jnp.bfloat16).reshape(1, 1, 1, STEPS, slot_total)
    return (final_field, prior_field, surface_accel, modal_state)


def solution(mesh):
    in_specs = (
        P(("groups", "tile"), "sub", "rep"),
        P(("groups", "tile"), "sub", "rep"),
        P(("groups", "tile"), "sub", "rep"),
        P(("groups", "tile", "sub", "rep")),
        P(("groups", "tile", "sub", "rep"), None),
        P("groups"),
        P("groups"),
        P(None, "groups"),
        P(("groups", "tile"), "sub", "rep", None),
        P(("groups", "tile"), "sub", "rep", None, None),
        P(("groups", "sub"), "rep", "tile"),
    )
    out_specs = (
        P(("groups", "tile"), "sub", "rep"),
        P(("groups", "tile"), "sub", "rep"),
        P(("groups", "tile"), "sub", "rep", None, None),
        P(None, ("groups", "tile", "sub", "rep")),
    )
    return jax.shard_map(body, mesh=mesh, in_specs=in_specs, out_specs=out_specs, check_vma=False)
```

profile of v0, /device:TPU:0, one launch (start us, length us, event | category | flops | bytes accessed | tf_op | source)
XLA Modules:
  0.0 172.1 jit_solution(446253793117891918)
XLA Ops:
  8.1 5.0 %collective-permute-start = (f32[2,4,16,128]{3,2,1,0:T(8,128)S(1)}, f32[2,4,16,128]{3,2,1,0:T(8,128)S(1)}, u32[]{:S(2)}, u32[]{:S(2)}) collective-permute-start(f32[2,4,16,128]{3,2,1,0:T(8,128)S(1)} %get-tuple-element.142), channel_id=1, source_target_pairs={{0,4},{4,8},{8,12},{1,5},{5,9},{9,13},{2,6},{6,10},{10,14},{3,7},{... | collective-permute-start | bytes 196616 | tf_op jit(solution)/shard_map/while/body/eval_jaxpr/ppermute | solution.py:21
  13.1 1.3 collective-permute-start.1
  15.2 4.5 %collective-permute-start.6 = (f32[4,16,128]{2,1,0:T(8,128)S(1)}, f32[4,16,128]{2,1,0:T(8,128)S(1)}, u32[]{:S(2)}, u32[]{:S(2)}) collective-permute-start(f32[4,16,128]{2,1,0:T(8,128)S(1)} %get-tuple-element.145), channel_id=1, source_target_pairs={{0,4},{4,8},{8,12},{1,5},{5,9},{9,13},{2,6},{6,10},{10,14},{3,7},{... | collective-permute-start | bytes 98312 | tf_op jit(solution)/shard_map/ppermute | solution.py:21
  19.7 1.3 collective-permute-start.7
  25.6 3.4 %collective-permute-start.8 = (f32[16,4,128]{2,1,0:T(4,128)S(1)}, f32[16,4,128]{2,1,0:T(4,128)S(1)}, u32[]{:S(2)}, u32[]{:S(2)}) collective-permute-start(f32[16,4,128]{2,1,0:T(4,128)S(1)} %get-tuple-element.140), channel_id=1, source_target_pairs={{0,2},{1,3},{4,6},{5,7},{8,10},{9,11},{12,14},{13,15},{16,18},{17,... | collective-permute-start | bytes 98312 | tf_op jit(solution)/shard_map/ppermute | solution.py:21
  29.0 1.3 collective-permute-start.9
  31.1 4.5 %collective-permute-start.2 = (f32[2,16,4,128]{3,2,1,0:T(4,128)S(1)}, f32[2,16,4,128]{3,2,1,0:T(4,128)S(1)}, u32[]{:S(2)}, u32[]{:S(2)}) collective-permute-start(f32[2,16,4,128]{3,2,1,0:T(4,128)S(1)} %get-tuple-element.136), channel_id=1, source_target_pairs={{0,2},{1,3},{4,6},{5,7},{8,10},{9,11},{12,14},{13,15},{16,18},{17,... | collective-permute-start | bytes 196616 | tf_op jit(solution)/shard_map/while/body/eval_jaxpr/ppermute | solution.py:21
  35.7 1.3 collective-permute-start.3
  37.2 1.3 collective-permute-start.10
  39.8 2.1 %collective-permute-done.3 = f32[2,16,4,128]{3,2,1,0:T(4,128)S(1)} collective-permute-done((f32[2,16,4,128]{3,2,1,0:T(4,128)S(1)}, f32[2,16,4,128]{3,2,1,0:T(4,128)S(1)}, u32[]{:S(2)}, u32[]{:S(2)}) %collective-permute-start.3) | collective-permute-done | bytes 65568 | tf_op jit(solution)/shard_map/while/body/eval_jaxpr/ppermute | solution.py:22
  42.1 1.3 collective-permute-start.4
  45.1 2.0 %collective-permute-done.5 = f32[2,16,24,4]{3,2,1,0:T(8,128)S(1)} collective-permute-done((f32[2,16,24,4]{3,2,1,0:T(8,128)S(1)}, f32[2,16,24,4]{3,2,1,0:T(8,128)S(1)}, u32[]{:S(2)}, u32[]{:S(2)}) %collective-permute-start.5) | collective-permute-done | bytes 12320 | tf_op jit(solution)/shard_map/while/body/eval_jaxpr/ppermute | solution.py:22
  47.7 1.4 slice_subtract_fusion
  51.9 2.5 %gather_fusion.2 = bf16[384]{0:T(512)(128)(2,1)S(1)} fusion(f32[16384]{0:T(1024)S(1)} %bitcast.42, s32[1024]{0:T(1024)S(1)} %pad_clamp_fusion), kind=kCustom, calls=%fused_computation.2.clone | custom fusion | bytes 3072 | tf_op jit(solution)/shard_map/while/body/eval_jaxpr/jit(_take)/gather | solution.py:132
  54.5 2.5 %gather_fusion.3 = bf16[384]{0:T(512)(128)(2,1)S(1)} fusion(f32[16384]{0:T(1024)S(1)} %bitcast.41, s32[1024]{0:T(1024)S(1)} %pad_clamp_fusion), kind=kCustom, calls=%fused_computation.3.clone | custom fusion | bytes 3072 | tf_op jit(solution)/shard_map/while/body/eval_jaxpr/jit(_take)/gather | solution.py:132
  57.0 2.8 %gather_fusion.1 = bf16[384]{0:T(512)(128)(2,1)S(1)} fusion(bf16[16384]{0:T(1024)(128)(2,1)S(1)} %bitcast.40, s32[1024]{0:T(1024)S(1)} %pad_clamp_fusion), kind=kCustom, calls=%fused_computation.1.clone | custom fusion | bytes 3072 | tf_op jit(solution)/shard_map/while/body/eval_jaxpr/jit(_take)/gather | solution.py:132
  59.9 2.8 %gather_fusion = bf16[384]{0:T(512)(128)(2,1)S(1)} fusion(bf16[16384]{0:T(1024)(128)(2,1)S(1)} %bitcast.39, s32[1024]{0:T(1024)S(1)} %pad_clamp_fusion), kind=kCustom, calls=%fused_computation.clone | custom fusion | bytes 3072 | tf_op jit(solution)/shard_map/while/body/eval_jaxpr/jit(_take)/gather | solution.py:132
  63.7 5.5 %all-to-all-start = ((bf16[4,4,96]{2,0,1:T(4,128)(2,1)}), bf16[4,4,96]{2,0,1:T(4,128)(2,1)S(1)}, u32[]{:S(2)}, u32[]{:S(2)}) async-start(bf16[4,4,96]{2,0,1:T(4,128)(2,1)} %copy.17), calls=%async_computation | async-start | bytes 8192 | tf_op jit(solution)/shard_map/all_to_all | solution.py:144
  69.3 5.6 %all-to-all-done = bf16[4,4,96]{2,0,1:T(4,128)(2,1)S(1)} async-done(((bf16[4,4,96]{2,0,1:T(4,128)(2,1)}), bf16[4,4,96]{2,0,1:T(4,128)(2,1)S(1)}, u32[]{:S(2)}, u32[]{:S(2)}) %all-to-all-start) | async-done | bytes 3104 | tf_op jit(solution)/shard_map/all_to_all | solution.py:144
  75.0 1.7 %convolution_bitcast_fusion = f32[2048,4]{1,0:T(8,128)} fusion(bf16[384,2048]{1,0:T(8,128)(2,1)S(1)} %copy-done, f32[4,384]{1,0:T(4,128)S(1)} %reshape.139, f32[384]{0:T(512)S(1)} %copy-done.6), kind=kOutput, calls=%fused_computation.6 | convolution fusion | flops 6294528 | bytes 1613312
  78.3 55.4 %reduce-scatter.4.cloned.1.call-done = f32[128,4]{1,0:T(8,128)} async-done(((f32[2048,4]{1,0:T(8,128)}), f32[128,4]{1,0:T(8,128)}) %reduce-scatter.4.cloned.1.call-update) | async-done | bytes 2064
  134.9 19.4 %all_gather.3 = bf16[4,2048]{1,0:T(4,128)(2,1)S(1)} all-gather(bf16[4,128]{1,0:T(4,128)(2,1)S(1)} %get-tuple-element.98), channel_id=1, replica_groups=mesh['groups'=2,'tile'=4,'sub'=2,'rep'=2] {'tile','sub','rep'}, dimensions={1}, use_global_device_ids=true | all-gather | bytes 17408 | tf_op jit(solution)/shard_map/all_gather | solution.py:161
  155.5 3.2 %all-to-all-start.1 = ((bf16[4,4,96]{2,0,1:T(4,128)(2,1)}), bf16[4,4,96]{2,0,1:T(4,128)(2,1)S(1)}, u32[]{:S(2)}, u32[]{:S(2)}) async-start(bf16[4,4,96]{2,0,1:T(4,128)(2,1)} %copy.19), calls=%async_computation.1 | async-start | bytes 8192 | tf_op jit(solution)/shard_map/all_to_all | solution.py:167
  159.3 5.0 %all-to-all-done.1 = bf16[4,4,96]{2,0,1:T(4,128)(2,1)S(1)} async-done(((bf16[4,4,96]{2,0,1:T(4,128)(2,1)}), bf16[4,4,96]{2,0,1:T(4,128)(2,1)S(1)}, u32[]{:S(2)}, u32[]{:S(2)}) %all-to-all-start.1) | async-done | bytes 3104 | tf_op jit(solution)/shard_map/all_to_all | solution.py:167
  (93 shorter events, 19.9 us)
Async XLA Ops:
  7.2 67.8 %copy-start = (bf16[384,2048]{1,0:T(8,128)(2,1)S(1)}, bf16[384,2048]{1,0:T(8,128)(2,1)}, u32[]{:S(2)}) copy-start(bf16[384,2048]{1,0:T(8,128)(2,1)} %param.19) | copy-start | bytes 4718596
  7.2 34.7 %copy-start.3 = (f32[8,16,128]{2,1,0:T(8,128)S(1)}, f32[8,16,128]{2,1,0:T(8,128)}, u32[]{:S(2)}) copy-start(f32[8,16,128]{2,1,0:T(8,128)} %param.15) | copy-start | bytes 196612
  7.2 34.7 %copy-start.4 = (f32[8,16,128]{2,1,0:T(8,128)S(1)}, f32[8,16,128]{2,1,0:T(8,128)}, u32[]{:S(2)}) copy-start(f32[8,16,128]{2,1,0:T(8,128)} %param.16) | copy-start | bytes 196612
  8.1 22.1 %collective-permute-start = (f32[2,4,16,128]{3,2,1,0:T(8,128)S(1)}, f32[2,4,16,128]{3,2,1,0:T(8,128)S(1)}, u32[]{:S(2)}, u32[]{:S(2)}) collective-permute-start(f32[2,4,16,128]{3,2,1,0:T(8,128)S(1)} %get-tuple-element.142), channel_id=1, source_target_pairs={{0,4},{4,8},{8,12},{1,5},{5,9},{9,13},{2,6},{6,10},{10,14},{3,7},{... | collective-permute-start | bytes 196616 | tf_op jit(solution)/shard_map/while/body/eval_jaxpr/ppermute | solution.py:21
  13.1 17.2 %collective-permute-start.1 = (f32[2,4,16,128]{3,2,1,0:T(8,128)S(1)}, f32[2,4,16,128]{3,2,1,0:T(8,128)S(1)}, u32[]{:S(2)}, u32[]{:S(2)}) collective-permute-start(f32[2,4,16,128]{3,2,1,0:T(8,128)S(1)} %get-tuple-element.143), channel_id=1, source_target_pairs={{4,0},{8,4},{12,8},{5,1},{9,5},{13,9},{6,2},{10,6},{14,10},{7,3},{... | collective-permute-start | bytes 196616 | tf_op jit(solution)/shard_map/while/body/eval_jaxpr/ppermute | solution.py:22
  15.2 9.1 %collective-permute-start.6 = (f32[4,16,128]{2,1,0:T(8,128)S(1)}, f32[4,16,128]{2,1,0:T(8,128)S(1)}, u32[]{:S(2)}, u32[]{:S(2)}) collective-permute-start(f32[4,16,128]{2,1,0:T(8,128)S(1)} %get-tuple-element.145), channel_id=1, source_target_pairs={{0,4},{4,8},{8,12},{1,5},{5,9},{9,13},{2,6},{6,10},{10,14},{3,7},{... | collective-permute-start | bytes 98312 | tf_op jit(solution)/shard_map/ppermute | solution.py:21
  19.7 5.8 %collective-permute-start.7 = (f32[4,16,128]{2,1,0:T(8,128)S(1)}, f32[4,16,128]{2,1,0:T(8,128)S(1)}, u32[]{:S(2)}, u32[]{:S(2)}) collective-permute-start(f32[4,16,128]{2,1,0:T(8,128)S(1)} %get-tuple-element.144), channel_id=1, source_target_pairs={{4,0},{8,4},{12,8},{5,1},{9,5},{13,9},{6,2},{10,6},{14,10},{7,3},{... | collective-permute-start | bytes 98312 | tf_op jit(solution)/shard_map/ppermute | solution.py:22
  25.6 11.4 %collective-permute-start.8 = (f32[16,4,128]{2,1,0:T(4,128)S(1)}, f32[16,4,128]{2,1,0:T(4,128)S(1)}, u32[]{:S(2)}, u32[]{:S(2)}) collective-permute-start(f32[16,4,128]{2,1,0:T(4,128)S(1)} %get-tuple-element.140), channel_id=1, source_target_pairs={{0,2},{1,3},{4,6},{5,7},{8,10},{9,11},{12,14},{13,15},{16,18},{17,... | collective-permute-start | bytes 98312 | tf_op jit(solution)/shard_map/ppermute | solution.py:21
  29.0 8.0 %collective-permute-start.9 = (f32[16,4,128]{2,1,0:T(4,128)S(1)}, f32[16,4,128]{2,1,0:T(4,128)S(1)}, u32[]{:S(2)}, u32[]{:S(2)}) collective-permute-start(f32[16,4,128]{2,1,0:T(4,128)S(1)} %get-tuple-element.141), channel_id=1, source_target_pairs={{2,0},{3,1},{6,4},{7,5},{10,8},{11,9},{14,12},{15,13},{18,16},{19,... | collective-permute-start | bytes 98312 | tf_op jit(solution)/shard_map/ppermute | solution.py:22
  31.1 8.6 %collective-permute-start.2 = (f32[2,16,4,128]{3,2,1,0:T(4,128)S(1)}, f32[2,16,4,128]{3,2,1,0:T(4,128)S(1)}, u32[]{:S(2)}, u32[]{:S(2)}) collective-permute-start(f32[2,16,4,128]{3,2,1,0:T(4,128)S(1)} %get-tuple-element.136), channel_id=1, source_target_pairs={{0,2},{1,3},{4,6},{5,7},{8,10},{9,11},{12,14},{13,15},{16,18},{17,... | collective-permute-start | bytes 196616 | tf_op jit(solution)/shard_map/while/body/eval_jaxpr/ppermute | solution.py:21
  35.7 6.2 %collective-permute-start.3 = (f32[2,16,4,128]{3,2,1,0:T(4,128)S(1)}, f32[2,16,4,128]{3,2,1,0:T(4,128)S(1)}, u32[]{:S(2)}, u32[]{:S(2)}) collective-permute-start(f32[2,16,4,128]{3,2,1,0:T(4,128)S(1)} %get-tuple-element.137), channel_id=1, source_target_pairs={{2,0},{3,1},{6,4},{7,5},{10,8},{11,9},{14,12},{15,13},{18,16},{19,... | collective-permute-start | bytes 196616 | tf_op jit(solution)/shard_map/while/body/eval_jaxpr/ppermute | solution.py:22
  37.2 7.6 %collective-permute-start.10 = (f32[16,24,4]{2,1,0:T(8,128)S(1)}, f32[16,24,4]{2,1,0:T(8,128)S(1)}, u32[]{:S(2)}, u32[]{:S(2)}) collective-permute-start(f32[16,24,4]{2,1,0:T(8,128)S(1)} %get-tuple-element.138), channel_id=1, source_target_pairs={{0,1},{2,3},{4,5},{6,7},{8,9},{10,11},{12,13},{14,15},{16,17},{18,... | collective-permute-start | bytes 18440 | tf_op jit(solution)/shard_map/ppermute | solution.py:21
  38.5 6.3 %collective-permute-start.11 = (f32[16,24,4]{2,1,0:T(8,128)S(1)}, f32[16,24,4]{2,1,0:T(8,128)S(1)}, u32[]{:S(2)}, u32[]{:S(2)}) collective-permute-start(f32[16,24,4]{2,1,0:T(8,128)S(1)} %get-tuple-element.139), channel_id=1, source_target_pairs={{1,0},{3,2},{5,4},{7,6},{9,8},{11,10},{13,12},{15,14},{17,16},{19,... | collective-permute-start | bytes 18440 | tf_op jit(solution)/shard_map/ppermute | solution.py:22
  42.1 2.9 %collective-permute-start.4 = (f32[2,16,24,4]{3,2,1,0:T(8,128)S(1)}, f32[2,16,24,4]{3,2,1,0:T(8,128)S(1)}, u32[]{:S(2)}, u32[]{:S(2)}) collective-permute-start(f32[2,16,24,4]{3,2,1,0:T(8,128)S(1)} %get-tuple-element.134), channel_id=1, source_target_pairs={{0,1},{2,3},{4,5},{6,7},{8,9},{10,11},{12,13},{14,15},{16,17},{18,... | collective-permute-start | bytes 36872 | tf_op jit(solution)/shard_map/while/body/eval_jaxpr/ppermute | solution.py:21
  43.4 3.6 %collective-permute-start.5 = (f32[2,16,24,4]{3,2,1,0:T(8,128)S(1)}, f32[2,16,24,4]{3,2,1,0:T(8,128)S(1)}, u32[]{:S(2)}, u32[]{:S(2)}) collective-permute-start(f32[2,16,24,4]{3,2,1,0:T(8,128)S(1)} %get-tuple-element.135), channel_id=1, source_target_pairs={{1,0},{3,2},{5,4},{7,6},{9,8},{11,10},{13,12},{15,14},{17,16},{19,... | collective-permute-start | bytes 36872 | tf_op jit(solution)/shard_map/while/body/eval_jaxpr/ppermute | solution.py:22
  50.5 1.1 copy-start.5
  51.9 7.9 %copy-start.1 = (f32[8,16,128]{2,1,0:T(8,128)}, f32[8,16,128]{2,1,0:T(8,128)S(1)}, u32[]{:S(2)}) copy-start(f32[8,16,128]{2,1,0:T(8,128)S(1)} %get-tuple-element.124) | copy-start | bytes 196612
  51.9 7.9 %copy-start.2 = (f32[8,16,128]{2,1,0:T(8,128)}, f32[8,16,128]{2,1,0:T(8,128)S(1)}, u32[]{:S(2)}) copy-start(f32[8,16,128]{2,1,0:T(8,128)S(1)} %get-tuple-element.125) | copy-start | bytes 196612
  54.5 20.5 %copy-start.6 = (f32[384]{0:T(512)S(1)}, f32[384]{0:T(512)}, u32[]{:S(2)}) copy-start(f32[384]{0:T(512)} %param.18) | copy-start | bytes 4612
  63.7 11.1 %all-to-all-start = ((bf16[4,4,96]{2,0,1:T(4,128)(2,1)}), bf16[4,4,96]{2,0,1:T(4,128)(2,1)S(1)}, u32[]{:S(2)}, u32[]{:S(2)}) async-start(bf16[4,4,96]{2,0,1:T(4,128)(2,1)} %copy.17), calls=%async_computation | async-start | bytes 8192 | tf_op jit(solution)/shard_map/all_to_all | solution.py:144
  69.3 64.4 %reduce-scatter.4.cloned.1.call-start = ((), (), s32[]{:S(2)}) async-start(), calls=%async_computation.3 | async-start | bytes 1114112
  155.5 8.8 %all-to-all-start.1 = ((bf16[4,4,96]{2,0,1:T(4,128)(2,1)}), bf16[4,4,96]{2,0,1:T(4,128)(2,1)S(1)}, u32[]{:S(2)}, u32[]{:S(2)}) async-start(bf16[4,4,96]{2,0,1:T(4,128)(2,1)} %copy.19), calls=%async_computation.1 | async-start | bytes 8192 | tf_op jit(solution)/shard_map/all_to_all | solution.py:167
Sparse Core Ops, SparseCore 0:
  76.9 56.7 reduce-scatter.3
where the time goes:
time: 173 us; the launch traced here: 172 us
  waiting for transfers between devices  70.5 us (41%)
  starting transfers between devices  36.6 us (21%)
  blocking collectives  19.4 us (11%)
  local copies, waits for them, and re-layouts  17 us (10%)
  between operations  15.2 us (9%)
  other arithmetic  9.79 us (6%)
  matrix products  3.65 us (2%)
    unnamed x2, waiting for transfers between devices  55.5 us
    ppermute x6, starting transfers between devices, extended(): before = lax.ppermute(last, axis, up)  20.1 us
    all_gather x1, blocking collectives, body(): lax.all_gather(modal_rounded, ('tile', 'sub', 'rep'), axis=1, tiled=True)  19.4 us
    gather x4, local copies, waits for them, and re-layouts, deep_block(): jnp.take(interior.reshape(-1), cell_index).astype(jnp.bfloat16)  10.7 us
    ppermute x6, starting transfers between devices, extended(): after = lax.ppermute(first, axis, down)  7.75 us
    all_to_all x1, waiting for transfers between devices, body(): lax.all_to_all(bucketed, 'tile', split_axis=1, concat_axis=1, tiled=True)  5.57 us
    all_to_all x1, starting transfers between devices, body(): lax.all_to_all(bucketed, 'tile', split_axis=1, concat_axis=1, tiled=True)  5.54 us
    all_to_all x1, waiting for transfers between devices, body(): lax.all_to_all(outgoing, 'tile', split_axis=1, concat_axis=1, tiled=True)  4.98 us
  transfers between devices with their start and end apart: 15, of which 6 were waited for; matrix products, arithmetic and copies ran while one was open for 5% of the time, Pallas kernels for 0%

commit v1 on v0

--- a/solution.py
+++ b/solution.py
@@ -1,6 +1,10 @@
+import functools
+
 import jax
 import jax.numpy as jnp
 from jax import lax
+from jax.experimental import pallas as pl
+from jax.experimental.pallas import tpu as pltpu
 from jax.sharding import PartitionSpec as P
 
 STEPS = 4
@@ -174,6 +178,500 @@
     surface_accel = surface.astype(jnp.bfloat16).reshape(1, 1, 1, STEPS, slot_total)
     return (final_field, prior_field, surface_accel, modal_state)
 
+LANES = 128
+MESH = pl.DeviceIdType.MESH
+
+
+def other_devices(tiles, subs, reps):
+    return [
+        (i, j, k)
+        for i in range(tiles)
+        for j in range(subs)
+        for k in range(reps)
+        if (i, j, k) != (0, 0, 0)
+    ]
+
+
+def dot(a, b, contract):
+    return lax.dot_general(a, b, ((contract[:1], contract[1:]), ((), ())), preferred_element_type=jnp.float32)
+
+
+def window_kernel(
+    tiles,
+    pressure_ref,
+    previous_ref,
+    courant_ref,
+    area_ref,
+    modes_hbm,
+    frequency_ref,
+    damping_ref,
+    start_ref,
+    cell_ref,
+    owner_ref,
+    count_ref,
+    final_ref,
+    prior_ref,
+    surface_ref,
+    state_ref,
+    modes,
+    field,
+    side_out,
+    low,
+    high,
+    side_in,
+    pair_in,
+    loads_out,
+    loads_in,
+    weighted,
+    force_out,
+    force_in,
+    accel_out,
+    accel_in,
+    back_out,
+    back_in,
+    modes_sem,
+    halo_send,
+    halo_recv,
+    loads_send,
+    loads_recv,
+    force_send,
+    force_recv,
+    accel_send,
+    accel_recv,
+    back_send,
+    back_recv,
+):
+    t, s, r = lax.axis_index("tile"), lax.axis_index("sub"), lax.axis_index("rep")
+    first, second, third = pressure_ref.shape
+    slots = cell_ref.shape[1]
+    bucket = slots // tiles
+    padded_rows = tiles * LANES
+    partners = other_devices(tiles, 2, 2)
+    share = state_ref.shape[1]
+    me = (t * 2 + s) * 2 + r
+
+    def place(offset):
+        i, j, k = offset
+        return (lax.rem(t + i, tiles), lax.rem(s + j, 2), lax.rem(r + k, 2))
+
+    def ident(where):
+        return {"tile": where[0], "sub": where[1], "rep": where[2]}
+
+    def linear(where):
+        return (where[0] * 2 + where[1]) * 2 + where[2]
+
+    barrier = pltpu.get_barrier_semaphore()
+    for offset in partners:
+        pl.semaphore_signal(barrier, inc=1, device_id=ident(place(offset)), device_id_type=MESH)
+
+    mode_copies = [
+        pltpu.make_async_copy(
+            modes_hbm.at[pl.ds(i * bucket, bucket)],
+            modes.at[pl.ds(i * LANES, bucket)],
+            modes_sem.at[i],
+        )
+        for i in range(tiles)
+    ]
+    for copy in mode_copies:
+        copy.start()
+
+    def row(value):
+        return jnp.where(s == 0, value[:, second - 1, :], value[:, 0, :])
+
+    p_now, p_before = pressure_ref[...], previous_ref[...]
+    side_out[0] = row(p_now)
+    side_out[1] = row(p_before)
+
+    def level(k):
+        return (pressure_ref, previous_ref)[k] if k < 2 else field.at[k - 2]
+
+    def remote(source, target, sems, index, where):
+        return pltpu.make_async_remote_copy(
+            src_ref=source,
+            dst_ref=target,
+            send_sem=sems[0].at[index],
+            recv_sem=sems[1].at[index],
+            device_id=where,
+            device_id_type=MESH,
+        )
+
+    halo = (halo_send, halo_recv)
+
+    def up_copy(k):
+        return remote(level(k).at[first - 1], low.at[k], halo, (k, 0), {"tile": jnp.minimum(t + 1, tiles - 1)})
+
+    def down_copy(k):
+        return remote(level(k).at[0], high.at[k], halo, (k, 1), {"tile": jnp.maximum(t - 1, 0)})
+
+    def side_copy(k):
+        return remote(side_out.at[k], side_in.at[k], halo, (k, 2), {"sub": 1 - s})
+
+    def pair_copy(k):
+        return remote(level(k), pair_in.at[k], halo, (k, 3), {"rep": 1 - r})
+
+    def send(k):
+        @pl.when(t < tiles - 1)
+        def _():
+            up_copy(k).start()
+
+        @pl.when(t > 0)
+        def _():
+            down_copy(k).start()
+
+        side_copy(k).start()
+        pair_copy(k).start()
+
+    def receive(k):
+        @pl.when(t > 0)
+        def _():
+            up_copy(k).wait_recv()
+
+        @pl.when(t < tiles - 1)
+        def _():
+            down_copy(k).wait_recv()
+
+        side_copy(k).wait_recv()
+        pair_copy(k).wait_recv()
+
+    def sent(k):
+        @pl.when(t < tiles - 1)
+        def _():
+            up_copy(k).wait_send()
+
+        @pl.when(t > 0)
+        def _():
+            down_copy(k).wait_send()
+
+        side_copy(k).wait_send()
+        pair_copy(k).wait_send()
+
+    pl.semaphore_wait(barrier, len(partners))
+    send(0)
+    send(1)
+
+    for i in range(tiles):
+        if bucket < LANES:
+            modes[i * LANES + bucket : (i + 1) * LANES, :] = jnp.zeros(
+                (LANES - bucket, modes.shape[1]), modes.dtype
+            )
+    weighted[...] = jnp.zeros_like(weighted)
+    owner = owner_ref[...]
+    cell = cell_ref[...]
+    lane = lax.broadcasted_iota(jnp.int32, (1, slots), 1)
+    live = lane < count_ref[...]
+    owner_live = jnp.where(live, owner, -1)
+    height = -(-tiles // 8) * 8
+    member = (
+        lax.broadcasted_iota(jnp.int32, (height, slots), 0) == owner_live
+    ).astype(jnp.float32)
+    earlier = (
+        lax.broadcasted_iota(jnp.int32, (slots, slots), 0)
+        < lax.broadcasted_iota(jnp.int32, (slots, slots), 1)
+    ).astype(jnp.float32).astype(jnp.bfloat16)
+    before = dot(member.astype(jnp.bfloat16), earlier, (1, 0))
+    rank = jnp.sum(before * member, axis=0, keepdims=True).astype(jnp.int32)
+    target = jnp.where(live, owner * LANES + rank, -1)
+    route = (
+        (lax.broadcasted_iota(jnp.int32, (padded_rows, slots), 0) == target)
+        .astype(jnp.float32)
+        .astype(jnp.bfloat16)
+    )
+    row_of = cell // third
+    lane_of = cell - row_of * third
+    pick_row = (
+        (lax.broadcasted_iota(jnp.int32, (first * second, slots), 0) == row_of)
+        .astype(jnp.float32)
+        .astype(jnp.bfloat16)
+    )
+    pick_lane = (
+        (lax.broadcasted_iota(jnp.int32, (third, slots), 0) == lane_of)
+        .astype(jnp.float32)
+        .astype(jnp.bfloat16)
+    )
+    at_row = dot(pick_row, route, (1, 1))
+    at_lane = dot(pick_lane, route, (1, 1)).astype(jnp.bfloat16)
+
+    courant = courant_ref[...]
+    at_first = lax.broadcasted_iota(jnp.int32, (first, 1, 1), 0)
+    at_second = lax.broadcasted_iota(jnp.int32, (1, second, third), 1)
+    at_third = lax.broadcasted_iota(jnp.int32, (1, second, third), 2)
+
+    def inner(p):
+        total = -6.0 * p
+        zero = jnp.zeros((1, second, third), jnp.float32)
+        total = total + jnp.concatenate([zero, p[:-1]], axis=0)
+        total = total + jnp.concatenate([p[1:], zero], axis=0)
+        total = total + jnp.where(at_second == 0, 0.0, pltpu.roll(p, 1, 1))
+        total = total + jnp.where(at_second == second - 1, 0.0, pltpu.roll(p, second - 1, 1))
+        total = total + jnp.where(at_third == 0, 0.0, pltpu.roll(p, 1, 2))
+        total = total + jnp.where(at_third == third - 1, 0.0, pltpu.roll(p, third - 1, 2))
+        return total
+
+    def outer(total, k):
+        below = jnp.where(t > 0, low[k], 0.0)
+        above = jnp.where(t < tiles - 1, high[k], 0.0)
+        edge = jnp.where(s == 0, second - 1, 0)
+        beside = jnp.where(at_second == edge, side_in[k][:, None, :], 0.0)
+        q = pair_in[k]
+        lane_edge = jnp.where(r == 0, third - 1, 0)
+        shifted = jnp.where(r == 0, pltpu.roll(q, third - 1, 2), pltpu.roll(q, 1, 2))
+        across = jnp.where(at_third == lane_edge, shifted, 0.0)
+        total = total + beside + across
+        return jnp.concatenate(
+            [total[:1] + below[None], total[1:-1], total[-1:] + above[None]], axis=0
+        )
+
+    lap_part, lap_before_part = inner(p_now), inner(p_before)
+    receive(0)
+    receive(1)
+    lap_before = outer(lap_before_part, 1)
+    lap = outer(lap_part, 0)
+    steps = STEPS
+    for n in range(steps):
+        change = p_now - p_before
+        driving = (
+            courant * lap
+            + viscous * (lap - lap_before)
+            + 2.0 * nonlinear * change * change
+        )
+        p_next = 2.0 * p_now - p_before + (1.0 + 2.0 * nonlinear * p_now) * driving
+        if n < steps - 1:
+            k = n + 2
+            field[n] = p_next
+            side_out[k] = row(p_next)
+            send(k)
+        else:
+            final_ref[...] = p_next
+            prior_ref[...] = p_now
+        chosen = dot(
+            p_next.reshape(first * second, third).astype(jnp.bfloat16), at_lane, (1, 0)
+        )
+        picked = jnp.sum(chosen * at_row, axis=0, keepdims=True)
+        for i in range(tiles):
+            loads_out[i, n : n + 1, :] = picked[:, i * LANES : (i + 1) * LANES]
+        if n < steps - 1:
+            lap_before = lap
+            part = inner(p_next)
+            receive(k)
+            lap = outer(part, k)
+            p_before, p_now = p_now, p_next
+
+    def tile_copy(source, target, sems, i):
+        to = lax.rem(t + i, tiles)
+        return remote(source.at[to], target.at[t], sems, i, {"tile": to})
+
+    loads_copies = [
+        tile_copy(loads_out, loads_in, (loads_send, loads_recv), i) for i in range(1, tiles)
+    ]
+    for copy in loads_copies[::-1]:
+        copy.start()
+    loads_in[t] = loads_out[t]
+    area = area_ref[...]
+    lane_row = lax.broadcasted_iota(jnp.int32, (1, LANES), 1)
+    areas = []
+    for i in range(tiles):
+        moved = pltpu.roll(area, (slots - i * bucket) % slots, 1) if i else area
+        areas.append(jnp.where(lane_row < bucket, moved[:, :LANES], 0.0))
+    for copy in mode_copies:
+        copy.wait()
+    for copy in loads_copies:
+        copy.wait_recv()
+    for i in range(tiles):
+        weighted[:steps, i * LANES : (i + 1) * LANES] = loads_in[i] * areas[i]
+    forces = dot(weighted[...].astype(jnp.bfloat16), modes[...], (1, 0))
+    devices = len(partners) + 1
+    for i in range(devices):
+        force_out[i] = forces[:steps, i * share : (i + 1) * share]
+
+    force_copies = [
+        remote(
+            force_out.at[linear(place(offset))],
+            force_in.at[i],
+            (force_send, force_recv),
+            i,
+            ident(place(offset)),
+        )
+        for i, offset in enumerate(partners)
+    ]
+    for copy in force_copies[::-1]:
+        copy.start()
+    begin = pl.multiple_of(me * share, LANES)
+    frequency = frequency_ref[:, pl.ds(begin, share)]
+    damping = damping_ref[:, pl.ds(begin, share)]
+    started = start_ref[:, pl.ds(begin, share)]
+    displace, velocity = started[0:1], started[1:2]
+    total = force_out[me]
+    for i, copy in enumerate(force_copies):
+        copy.wait_recv()
+        total = total + force_in[i]
+    for n in range(steps):
+        accel = (
+            total[n : n + 1]
+            - 2.0 * damping * frequency * velocity
+            - frequency * frequency * displace
+        )
+        velocity = velocity + accel
+        displace = displace + velocity
+        accel_out[n : n + 1, :] = accel.astype(jnp.bfloat16).astype(jnp.float32)
+    accel_copies = [
+        remote(accel_out, accel_in.at[me], (accel_send, accel_recv), i, ident(place(offset)))
+        for i, offset in enumerate(partners)
+    ]
+    for copy in accel_copies[::-1]:
+        copy.start()
+    state_ref[0:1, :] = displace
+    state_ref[1:2, :] = velocity
+    accel_in[me] = accel_out[...]
+    for copy in accel_copies:
+        copy.wait_recv()
+    accels = jnp.concatenate([accel_in[i] for i in range(devices)], axis=1)
+    node = dot(accels.astype(jnp.bfloat16), modes[...], (1, 1))
+    node = node.astype(jnp.bfloat16).astype(jnp.float32)
+    for i in range(tiles):
+        back_out[i] = node[:, i * LANES : (i + 1) * LANES]
+    back_copies = [
+        tile_copy(back_out, back_in, (back_send, back_recv), i) for i in range(1, tiles)
+    ]
+    for copy in back_copies[::-1]:
+        copy.start()
+    back_in[t] = back_out[t]
+    for k in range(steps + 1):
+        sent(k)
+    for copy in loads_copies + force_copies + accel_copies:
+        copy.wait_send()
+    for copy in back_copies:
+        copy.wait_recv()
+    returned = jnp.concatenate([back_in[i] for i in range(tiles)], axis=1)
+    surface = dot(returned.astype(jnp.bfloat16), route, (1, 0))
+    surface_ref[...] = surface.astype(jnp.bfloat16)
+    for copy in back_copies:
+        copy.wait_send()
+
+
+def fused_body(
+    pressure,
+    previous_pressure,
+    courant_square,
+    node_area,
+    mode_shapes,
+    frequency,
+    damping_ratio,
+    modal_start,
+    slot_cell,
+    slot_owner,
+    surface_count,
+):
+    tiles = lax.axis_size("tile")
+    devices = tiles * lax.axis_size("sub") * lax.axis_size("rep")
+    first, second, third = pressure.shape
+    slots = slot_cell.shape[-1]
+    modes = mode_shapes.shape[1]
+    share = modes // devices
+    f32 = jnp.float32
+    levels = STEPS + 1
+    vmem = pl.BlockSpec(memory_space=pltpu.VMEM)
+    dma = pltpu.SemaphoreType.DMA
+    outputs = pl.pallas_call(
+        functools.partial(window_kernel, tiles),
+        out_shape=(
+            jax.ShapeDtypeStruct(pressure.shape, f32),
+            jax.ShapeDtypeStruct(pressure.shape, f32),
+            jax.ShapeDtypeStruct((STEPS, slots), jnp.bfloat16),
+            jax.ShapeDtypeStruct((2, share), f32),
+        ),
+        in_specs=[vmem] * 4 + [pl.BlockSpec(memory_space=pl.ANY)] + [vmem] * 6,
+        out_specs=(vmem,) * 4,
+        scratch_shapes=[
+            pltpu.VMEM((tiles * LANES, modes), mode_shapes.dtype),
+            pltpu.VMEM((STEPS - 1, first, second, third), f32),
+            pltpu.VMEM((levels, first, third), f32),
+            pltpu.VMEM((levels, second, third), f32),
+            pltpu.VMEM((levels, second, third), f32),
+            pltpu.VMEM((levels, first, third), f32),
+            pltpu.VMEM((levels, first, second, third), f32),
+            pltpu.VMEM((tiles, STEPS, LANES), f32),
+            pltpu.VMEM((tiles, STEPS, LANES), f32),
+            pltpu.VMEM((8, tiles * LANES), f32),
+            pltpu.VMEM((devices, STEPS, share), f32),
+            pltpu.VMEM((devices, STEPS, share), f32),
+            pltpu.VMEM((STEPS, share), f32),
+            pltpu.VMEM((devices, STEPS, share), f32),
+            pltpu.VMEM((tiles, STEPS, LANES), f32),
+            pltpu.VMEM((tiles, STEPS, LANES), f32),
+            dma((tiles,)),
+            dma((levels, 4)),
+            dma((levels, 4)),
+            dma((tiles,)),
+            dma((tiles,)),
+            dma((devices,)),
+            dma((devices,)),
+            dma((devices,)),
+            dma((devices,)),
+            dma((tiles,)),
+            dma((tiles,)),
+        ],
+        compiler_params=pltpu.CompilerParams(collective_id=0, has_side_effects=True),
+        name="window",
+    )(
+        pressure,
+        previous_pressure,
+        courant_square,
+        node_area.reshape(1, slots),
+        mode_shapes,
+        frequency.reshape(1, modes),
+        damping_ratio.reshape(1, modes),
+        modal_start,
+        slot_cell.reshape(1, slots),
+        slot_owner.reshape(1, slots),
+        surface_count.reshape(1, 1),
+    )
+    final_field, prior_field, surface, state = outputs
+    return (final_field, prior_field, surface.reshape(1, 1, 1, STEPS, slots), state)
+
+
+def pick_body(
+    pressure,
+    previous_pressure,
+    courant_square,
+    node_area,
+    mode_shapes,
+    frequency,
+    damping_ratio,
+    modal_start,
+    slot_cell,
+    slot_owner,
+    surface_count,
+):
+    tiles, subs, reps = (lax.axis_size(axis) for axis in ("tile", "sub", "rep"))
+    bucket = slot_cell.shape[-1] // tiles
+    modes = mode_shapes.shape[1]
+    fits = (
+        subs == 2
+        and reps == 2
+        and tiles > 1
+        and pressure.shape[2] == LANES
+        and pressure.shape[1] % 8 == 0
+        and pressure.shape[0] > 1
+        and max(pressure.shape[0] * pressure.shape[1], LANES) <= 256
+        and bucket <= LANES
+        and bucket % 16 == 0
+        and slot_cell.shape[-1] % LANES == 0
+        and modes % (tiles * subs * reps * LANES) == 0
+    )
+    return (fused_body if fits else body)(
+        pressure,
+        previous_pressure,
+        courant_square,
+        node_area,
+        mode_shapes,
+        frequency,
+        damping_ratio,
+        modal_start,
+        slot_cell,
+        slot_owner,
+        surface_count,
+    )
+
 
 def solution(mesh):
     in_specs = (
@@ -195,4 +693,5 @@
         P(("groups", "tile"), "sub", "rep", None, None),
         P(None, ("groups", "tile", "sub", "rep")),
     )
-    return jax.shard_map(body, mesh=mesh, in_specs=in_specs, out_specs=out_specs, check_vma=False)
+    return jax.shard_map(
+        pick_body, mesh=mesh, in_specs=in_specs, out_specs=out_specs, check_vma=False)

time: 173 us -> 44.7 us (0.26)
  waiting for transfers between devices: 70.5 us -> 0 us
  starting transfers between devices: 36.6 us -> 0 us
  Pallas kernels: 0 us -> 36.4 us
  blocking collectives: 19.4 us -> 0 us
  between operations: 15.2 us -> 1.29 us
  local copies, waits for them, and re-layouts: 17 us -> 6.67 us
  other arithmetic: 9.79 us -> 0 us
  matrix products: 3.65 us -> 0 us
    unnamed x2 -> x0, waiting for transfers between devices: 55.5 us -> none
    pallas_call x0 -> x1, Pallas kernels: none -> 36.4 us  [fused_body(): pl.pallas_call(functools.partial(window_kernel, tiles), out_shape=(jax.Sh...]
    ppermute x12 -> x0, starting transfers between devices: 27.8 us -> none  [the longest x6 20.1 us: extended(): before = lax.ppermute(last, axis, up)]
    all_gather x1 -> x0, blocking collectives: 19.4 us -> none  [body(): lax.all_gather(modal_rounded, ('tile', 'sub', 'rep'), axis=1, tiled=True)]
    gather x4 -> x0, local copies, waits for them, and re-layouts: 10.7 us -> none  [deep_block(): jnp.take(interior.reshape(-1), cell_index).astype(jnp.bfloat16)]
    all_to_all x2 -> x0, waiting for transfers between devices: 10.5 us -> none  [the longest x1 5.57 us: body(): lax.all_to_all(bucketed, 'tile', split_axis=1, concat_axis=1, tiled=True)]
    all_to_all x2 -> x0, starting transfers between devices: 8.79 us -> none  [the longest x1 5.54 us: body(): lax.all_to_all(bucketed, 'tile', split_axis=1, concat_axis=1, tiled=True)]
    ppermute x12 -> x0, waiting for transfers between devices: 4.48 us -> none  [the longest x6 4.46 us: extended(): after = lax.ppermute(first, axis, down)]
  transfers between devices with their start and end apart: 15 -> 0, of which waited for: 6 -> 0; matrix products, arithmetic and copies ran while one was open for 5% -> 0% of each run, Pallas kernels for 0% -> 0%
where the time goes in v1:
time: 44.7 us; the launch traced here: 44.4 us
  Pallas kernels  36.4 us (81%)
  local copies, waits for them, and re-layouts  6.67 us (15%)
  between operations  1.29 us (3%)
    pallas_call x1, Pallas kernels, fused_body(): pl.pallas_call(functools.partial(window_kernel, tiles), out_shape=(jax.Sh...  36.4 us
    unnamed x4, local copies, waits for them, and re-layouts  5.43 us
    reshape x1, local copies, waits for them, and re-layouts, fused_body(): node_area.reshape(1, slots)  1.25 us

profile of v1, /device:TPU:0, one launch (start us, length us, event | category | flops | bytes accessed | tf_op | source)
XLA Modules:
  0.0 44.4 jit_solution(8586589990521818857)
XLA Ops:
  1.3 1.2 %reshape.29.area_ref = f32[1,384]{1,0:T(1,128)} reshape(f32[384]{0:T(512)} %param.14) | data formatting | bytes 3072 | tf_op jit(solution)/shard_map/reshape | solution.py:619
  2.5 36.4 %window.1 = (f32[8,16,128]{2,1,0:T(8,128)}, f32[8,16,128]{2,1,0:T(8,128)}, bf16[4,384]{1,0:T(4,128)(2,1)}, f32[2,128]{1,0:T(2,128)}) custom-call(f32[8,16,128]{2,1,0:T(8,128)} %pressure_ref.1, f32[8,16,128]{2,1,0:T(8,128)} %previous_ref.1, f32[8,16,128]{2,1,0:T(8,128)} %courant_ref.1, f32[1,384]{1,0:T(1,128)} %reshape.29.area_ref, ...), custom_call_target="tpu_custom_call" | custom-call | tf_op jit(solution)/shard_map/window/pallas_call | solution.py:574
  39.0 1.5 %copy.20 = f32[8,16,128]{2,1,0:T(8,128)} copy(f32[8,16,128]{2,1,0:T(8,128)} %get-tuple-element.16) | data formatting | bytes 131072
  40.4 1.5 %copy.21 = f32[8,16,128]{2,1,0:T(8,128)} copy(f32[8,16,128]{2,1,0:T(8,128)} %get-tuple-element.17) | data formatting | bytes 131072
  41.9 1.3 %copy.22 = bf16[1,1,1,4,384]{4,3,2,1,0:T(4,128)(2,1)} copy(bf16[1,1,1,4,384]{4,3,2,1,0:T(4,128)(2,1)} %bitcast.9) | data formatting | bytes 6144
  43.2 1.2 %copy.23 = f32[2,128]{1,0:T(2,128)} copy(f32[2,128]{1,0:T(2,128)} %get-tuple-element.19) | data formatting | bytes 2048

commit v2 on v1

--- a/solution.py
+++ b/solution.py
@@ -198,21 +198,31 @@
 
 def window_kernel(
     tiles,
+    pressure_hbm,
+    previous_hbm,
+    courant_hbm,
+    area_hbm,
+    modes_hbm,
+    frequency_hbm,
+    damping_hbm,
+    start_hbm,
+    cell_hbm,
+    owner_hbm,
+    count_hbm,
+    final_ref,
+    prior_ref,
+    surface_ref,
+    state_ref,
     pressure_ref,
     previous_ref,
     courant_ref,
     area_ref,
-    modes_hbm,
     frequency_ref,
     damping_ref,
     start_ref,
     cell_ref,
     owner_ref,
     count_ref,
-    final_ref,
-    prior_ref,
-    surface_ref,
-    state_ref,
     modes,
     field,
     side_out,
@@ -240,6 +250,7 @@
     accel_recv,
     back_send,
     back_recv,
+    input_sem,
 ):
     t, s, r = lax.axis_index("tile"), lax.axis_index("sub"), lax.axis_index("rep")
     first, second, third = pressure_ref.shape
@@ -272,12 +283,32 @@
         )
         for i in range(tiles)
     ]
+    inputs = [
+        (pressure_hbm, pressure_ref),
+        (previous_hbm, previous_ref),
+        (courant_hbm, courant_ref),
+        (area_hbm, area_ref),
+        (frequency_hbm, frequency_ref),
+        (damping_hbm, damping_ref),
+        (start_hbm, start_ref),
+        (cell_hbm, cell_ref),
+        (owner_hbm, owner_ref),
+        (count_hbm, count_ref),
+    ]
+    input_copies = [
+        pltpu.make_async_copy(source, held, input_sem.at[i])
+        for i, (source, held) in enumerate(inputs)
+    ]
+    for copy in input_copies:
+        copy.start()
     for copy in mode_copies:
         copy.start()
 
     def row(value):
         return jnp.where(s == 0, value[:, second - 1, :], value[:, 0, :])
 
+    for copy in input_copies:
+        copy.wait()
     p_now, p_before = pressure_ref[...], previous_ref[...]
     side_out[0] = row(p_now)
     side_out[1] = row(p_before)
@@ -358,7 +389,7 @@
     owner = owner_ref[...]
     cell = cell_ref[...]
     lane = lax.broadcasted_iota(jnp.int32, (1, slots), 1)
-    live = lane < count_ref[...]
+    live = lane < count_ref[0]
     owner_live = jnp.where(live, owner, -1)
     height = -(-tiles // 8) * 8
     member = (
@@ -466,7 +497,7 @@
     for copy in loads_copies[::-1]:
         copy.start()
     loads_in[t] = loads_out[t]
-    area = area_ref[...]
+    area = area_ref[...].reshape(1, slots)
     lane_row = lax.broadcasted_iota(jnp.int32, (1, LANES), 1)
     areas = []
     for i in range(tiles):
@@ -548,6 +579,18 @@
         copy.wait_send()
 
 
+def place_kernel(*refs):
+    sources, targets, sems = refs[:4], refs[4:8], refs[8]
+    copies = [
+        pltpu.make_async_copy(source, target, sems.at[i])
+        for i, (source, target) in enumerate(zip(sources, targets))
+    ]
+    for copy in copies:
+        copy.start()
+    for copy in copies:
+        copy.wait()
+
+
 def fused_body(
     pressure,
     previous_pressure,
@@ -571,17 +614,28 @@
     levels = STEPS + 1
     vmem = pl.BlockSpec(memory_space=pltpu.VMEM)
     dma = pltpu.SemaphoreType.DMA
+    shapes = (
+        jax.ShapeDtypeStruct(pressure.shape, f32),
+        jax.ShapeDtypeStruct(pressure.shape, f32),
+        jax.ShapeDtypeStruct((STEPS, slots), jnp.bfloat16),
+        jax.ShapeDtypeStruct((2, share), f32),
+    )
     outputs = pl.pallas_call(
         functools.partial(window_kernel, tiles),
-        out_shape=(
-            jax.ShapeDtypeStruct(pressure.shape, f32),
-            jax.ShapeDtypeStruct(pressure.shape, f32),
-            jax.ShapeDtypeStruct((STEPS, slots), jnp.bfloat16),
-            jax.ShapeDtypeStruct((2, share), f32),
-        ),
-        in_specs=[vmem] * 4 + [pl.BlockSpec(memory_space=pl.ANY)] + [vmem] * 6,
+        out_shape=tuple(pltpu.VMEM(shape.shape, shape.dtype) for shape in shapes),
+        in_specs=[pl.BlockSpec(memory_space=pl.ANY)] * 11,
         out_specs=(vmem,) * 4,
         scratch_shapes=[
+            pltpu.VMEM(pressure.shape, f32),
+            pltpu.VMEM(pressure.shape, f32),
+            pltpu.VMEM(pressure.shape, f32),
+            pltpu.VMEM(node_area.shape, f32),
+            pltpu.VMEM((1, modes), f32),
+            pltpu.VMEM((1, modes), f32),
+            pltpu.VMEM((2, modes), f32),
+            pltpu.VMEM((1, slots), jnp.int32),
+            pltpu.VMEM((1, slots), jnp.int32),
+            pltpu.VMEM((1, 1, 1), jnp.int32),
             pltpu.VMEM((tiles * LANES, modes), mode_shapes.dtype),
             pltpu.VMEM((STEPS - 1, first, second, third), f32),
             pltpu.VMEM((levels, first, third), f32),
@@ -609,6 +663,7 @@
             dma((devices,)),
             dma((tiles,)),
             dma((tiles,)),
+            dma((10,)),
         ],
         compiler_params=pltpu.CompilerParams(collective_id=0, has_side_effects=True),
         name="window",
@@ -616,16 +671,23 @@
         pressure,
         previous_pressure,
         courant_square,
-        node_area.reshape(1, slots),
+        node_area,
         mode_shapes,
         frequency.reshape(1, modes),
         damping_ratio.reshape(1, modes),
         modal_start,
         slot_cell.reshape(1, slots),
         slot_owner.reshape(1, slots),
-        surface_count.reshape(1, 1),
-    )
-    final_field, prior_field, surface, state = outputs
+        surface_count,
+    )
+    final_field, prior_field, surface, state = pl.pallas_call(
+        place_kernel,
+        out_shape=shapes,
+        in_specs=[vmem] * 4,
+        out_specs=(pl.BlockSpec(memory_space=pl.ANY),) * 4,
+        scratch_shapes=[dma((4,))],
+        name="placed",
+    )(*(pltpu.with_memory_space_constraint(x, pltpu.VMEM) for x in outputs))
     return (final_field, prior_field, surface.reshape(1, 1, 1, STEPS, slots), state)
 
 

time: 44.7 us -> 37.1 us (0.83)
  local copies, waits for them, and re-layouts: 6.67 us -> 0 us
  Pallas kernels: 36.4 us -> 35.7 us
    unnamed x4 -> x0, local copies, waits for them, and re-layouts: 5.43 us -> none
    reshape x1 -> x0, local copies, waits for them, and re-layouts: 1.25 us -> none  [fused_body(): node_area.reshape(1, slots)]
    pallas_call x1 -> x2, Pallas kernels: 36.4 us -> 35.7 us  [the longest x1 35 us: fused_body(): pl.pallas_call(functools.partial(window_kernel, tiles), out_shape=tuple((...]
where the time goes in v2:
time: 37.1 us; the launch traced here: 37 us
  Pallas kernels  35.7 us (96%)
  between operations  1.29 us (3%)
    pallas_call x1, Pallas kernels, fused_body(): pl.pallas_call(functools.partial(window_kernel, tiles), out_shape=tuple((...  35 us

profile of v2, /device:TPU:0, one launch (start us, length us, event | category | flops | bytes accessed | tf_op | source)
XLA Modules:
  0.0 37.0 jit_solution(8116541903019243243)
XLA Ops:
  1.3 35.0 %window.1 = (f32[8,16,128]{2,1,0:T(8,128)S(1)}, f32[8,16,128]{2,1,0:T(8,128)S(1)}, bf16[4,384]{1,0:T(4,128)(2,1)S(1)}, f32[2,128]{1,0:T(2,128)S(1)}) custom-call(f32[8,16,128]{2,1,0:T(8,128)} %pressure_hbm.1, f32[8,16,128]{2,1,0:T(8,128)} %previous_hbm.1, f32[8,16,128]{2,1,0:T(8,128)} %courant_hbm.1, f32[384]{0:T(512)} %area_hbm.1, ...), custom_call_target="tpu_custom_call" | custom-call | tf_op jit(solution)/shard_map/window/pallas_call | solution.py:623
  36.3 0.7 %placed.1 = (f32[8,16,128]{2,1,0:T(8,128)}, f32[8,16,128]{2,1,0:T(8,128)}, bf16[4,384]{1,0:T(4,128)(2,1)}, f32[2,128]{1,0:T(2,128)}) custom-call(f32[8,16,128]{2,1,0:T(8,128)S(1)} %get-tuple-element.12.refs_0_, f32[8,16,128]{2,1,0:T(8,128)S(1)} %get-tuple-element.13.refs_1_, bf16[4,384]{1,0:T(4,128)(2,1)S(1)} %get-tuple-element.14.refs_2_, ...), custom_call_target="tpu_custom_call" | custom-call | tf_op jit(solution)/shard_map/placed/pallas_call | solution.py:683

commit v3 on v2

--- a/solution.py
+++ b/solution.py
@@ -226,10 +226,14 @@
     modes,
     field,
     side_out,
+    corner_out,
     low,
     high,
     side_in,
     pair_in,
+    corner_in,
+    layer_in,
+    across_in,
     loads_out,
     loads_in,
     weighted,
@@ -304,17 +308,29 @@
     for copy in mode_copies:
         copy.start()
 
-    def row(value):
+    def near(value):
         return jnp.where(s == 0, value[:, second - 1, :], value[:, 0, :])
+
+    def next_near(value):
+        return jnp.where(s == 0, value[:, second - 2, :], value[:, 1, :])
+
+    def stage(k, value):
+        rows = near(value)
+        side_out[k, 0] = rows
+        side_out[k, 1] = next_near(value)
+        corner_out[k, 0] = rows[:1]
+        corner_out[k, 1] = rows[first - 1 :]
 
     for copy in input_copies:
         copy.wait()
     p_now, p_before = pressure_ref[...], previous_ref[...]
-    side_out[0] = row(p_now)
-    side_out[1] = row(p_before)
+    courant = courant_ref[...]
+    stage(0, p_now)
+    stage(1, p_before)
+    stage(4, courant)
 
     def level(k):
-        return (pressure_ref, previous_ref)[k] if k < 2 else field.at[k - 2]
+        return (pressure_ref, previous_ref, field.at[0], field.at[1], courant_ref)[k]
 
     def remote(source, target, sems, index, where):
         return pltpu.make_async_remote_copy(
@@ -326,59 +342,56 @@
             device_id_type=MESH,
         )
 
-    halo = (halo_send, halo_recv)
-
-    def up_copy(k):
-        return remote(level(k).at[first - 1], low.at[k], halo, (k, 0), {"tile": jnp.minimum(t + 1, tiles - 1)})
-
-    def down_copy(k):
-        return remote(level(k).at[0], high.at[k], halo, (k, 1), {"tile": jnp.maximum(t - 1, 0)})
-
-    def side_copy(k):
-        return remote(side_out.at[k], side_in.at[k], halo, (k, 2), {"sub": 1 - s})
-
-    def pair_copy(k):
-        return remote(level(k), pair_in.at[k], halo, (k, 3), {"rep": 1 - r})
-
-    def send(k):
+    up = {"tile": jnp.minimum(t + 1, tiles - 1)}
+    down = {"tile": jnp.maximum(t - 1, 0)}
+    beside_me, pair = {"sub": 1 - s}, {"rep": 1 - r}
+
+    def piece(k, m):
+        source, target, where = (
+            (level(k).at[pl.ds(first - 2, 2)], low.at[k], up),
+            (level(k).at[pl.ds(0, 2)], high.at[k], down),
+            (side_out.at[k], side_in.at[k], beside_me),
+            (level(k), pair_in.at[k], pair),
+            (corner_out.at[k, 1], corner_in.at[k, 0], up | beside_me),
+            (corner_out.at[k, 0], corner_in.at[k, 1], down | beside_me),
+            (level(k).at[first - 1], layer_in.at[k, 0], up | pair),
+            (level(k).at[0], layer_in.at[k, 1], down | pair),
+            (side_out.at[k, 0], across_in.at[k], beside_me | pair),
+        )[m]
+        return remote(source, target, (halo_send, halo_recv), (k, m), where)
+
+    def pieces(k):
+        return (0, 1, 2, 3) if k == 4 else (0, 1, 6, 7, 4, 5, 8, 2, 3)
+
+    def each(ks, upward, act):
+        todo = [(k, m) for k in ks for m in pieces(k)]
+
+        def run(chosen):
+            for k, m in todo:
+                if m in chosen:
+                    act(piece(k, m))
+
         @pl.when(t < tiles - 1)
         def _():
-            up_copy(k).start()
+            run((0, 4, 6) if upward else (1, 5, 7))
 
         @pl.when(t > 0)
         def _():
-            down_copy(k).start()
-
-        side_copy(k).start()
-        pair_copy(k).start()
-
-    def receive(k):
-        @pl.when(t > 0)
-        def _():
-            up_copy(k).wait_recv()
-
-        @pl.when(t < tiles - 1)
-        def _():
-            down_copy(k).wait_recv()
-
-        side_copy(k).wait_recv()
-        pair_copy(k).wait_recv()
-
-    def sent(k):
-        @pl.when(t < tiles - 1)
-        def _():
-            up_copy(k).wait_send()
-
-        @pl.when(t > 0)
-        def _():
-            down_copy(k).wait_send()
-
-        side_copy(k).wait_send()
-        pair_copy(k).wait_send()
+            run((1, 5, 7) if upward else (0, 4, 6))
+
+        run((2, 3, 8))
+
+    def send(ks):
+        each(ks, True, lambda copy: copy.start())
+
+    def receive(ks):
+        each(ks, False, lambda copy: copy.wait_recv())
+
+    def sent(ks):
+        each(ks, True, lambda copy: copy.wait_send())
 
     pl.semaphore_wait(barrier, len(partners))
-    send(0)
-    send(1)
+    send((0, 1, 4))
 
     for i in range(tiles):
         if bucket < LANES:
@@ -422,70 +435,119 @@
     at_row = dot(pick_row, route, (1, 1))
     at_lane = dot(pick_lane, route, (1, 1)).astype(jnp.bfloat16)
 
-    courant = courant_ref[...]
-    at_first = lax.broadcasted_iota(jnp.int32, (first, 1, 1), 0)
     at_second = lax.broadcasted_iota(jnp.int32, (1, second, third), 1)
-    at_third = lax.broadcasted_iota(jnp.int32, (1, second, third), 2)
-
-    def inner(p):
-        total = -6.0 * p
-        zero = jnp.zeros((1, second, third), jnp.float32)
-        total = total + jnp.concatenate([zero, p[:-1]], axis=0)
-        total = total + jnp.concatenate([p[1:], zero], axis=0)
+    at_third = lax.broadcasted_iota(jnp.int32, (1, 1, third), 2)
+    edge_row = jnp.where(s == 0, second - 1, 0)
+
+    def along_lanes(p, q, half, lanes):
+        axis = p.ndim - 1
+        total = jnp.where(lanes == 0, 0.0, pltpu.roll(p, 1, axis))
+        total = total + jnp.where(lanes == third - 1, 0.0, pltpu.roll(p, third - 1, axis))
+        edge = jnp.where(half == 0, third - 1, 0)
+        shifted = jnp.where(half == 0, pltpu.roll(q, third - 1, axis), pltpu.roll(q, 1, axis))
+        return total + jnp.where(lanes == edge, shifted, 0.0)
+
+    def lap_block(p, below, above, beside, q, half):
+        total = along_lanes(p, q, half, at_third) - 6.0 * p
+        if p.shape[0] > 1:
+            below = jnp.concatenate([below, p[:-1]], axis=0)
+            above = jnp.concatenate([p[1:], above], axis=0)
+        total = total + below + above
         total = total + jnp.where(at_second == 0, 0.0, pltpu.roll(p, 1, 1))
         total = total + jnp.where(at_second == second - 1, 0.0, pltpu.roll(p, second - 1, 1))
-        total = total + jnp.where(at_third == 0, 0.0, pltpu.roll(p, 1, 2))
-        total = total + jnp.where(at_third == third - 1, 0.0, pltpu.roll(p, third - 1, 2))
-        return total
-
-    def outer(total, k):
-        below = jnp.where(t > 0, low[k], 0.0)
-        above = jnp.where(t < tiles - 1, high[k], 0.0)
-        edge = jnp.where(s == 0, second - 1, 0)
-        beside = jnp.where(at_second == edge, side_in[k][:, None, :], 0.0)
-        q = pair_in[k]
-        lane_edge = jnp.where(r == 0, third - 1, 0)
-        shifted = jnp.where(r == 0, pltpu.roll(q, third - 1, 2), pltpu.roll(q, 1, 2))
-        across = jnp.where(at_third == lane_edge, shifted, 0.0)
-        total = total + beside + across
-        return jnp.concatenate(
-            [total[:1] + below[None], total[1:-1], total[-1:] + above[None]], axis=0
-        )
-
-    lap_part, lap_before_part = inner(p_now), inner(p_before)
-    receive(0)
-    receive(1)
-    lap_before = outer(lap_before_part, 1)
-    lap = outer(lap_part, 0)
+        return total + jnp.where(at_second == edge_row, beside[:, None, :], 0.0)
+
+    at_layer = lax.broadcasted_iota(jnp.int32, (first, third), 0)
+    at_lane_side = lax.broadcasted_iota(jnp.int32, (1, third), 1)
+
+    def lap_side(g, inward, outward, below, above, q):
+        total = along_lanes(g, q, r, at_lane_side) - 6.0 * g
+        total = total + inward + outward
+        total = total + jnp.where(at_layer == 0, below, pltpu.roll(g, 1, 0))
+        return total + jnp.where(at_layer == first - 1, above, pltpu.roll(g, first - 1, 0))
+
+    has_below, has_above = t > 0, t < tiles - 1
+
+    def arrived(k):
+        return dict(
+            low=jnp.where(has_below, low[k], 0.0),
+            high=jnp.where(has_above, high[k], 0.0),
+            side=side_in[k],
+            pair=pair_in[k],
+            corner_low=jnp.where(has_below, corner_in[k, 0], 0.0),
+            corner_high=jnp.where(has_above, corner_in[k, 1], 0.0),
+            layer_low=jnp.where(has_below, layer_in[k, 0], 0.0)[None],
+            layer_high=jnp.where(has_above, layer_in[k, 1], 0.0)[None],
+            across=across_in[k],
+        )
+
+    def lap_own(p, h):
+        return lap_block(p, h["low"][1:], h["high"][:1], h["side"][0], h["pair"], r)
+
+    def lap_rim(p, h):
+        low_rim = lap_block(
+            h["low"][1:], h["low"][:1], p[:1], h["corner_low"], h["layer_low"], r
+        )
+        high_rim = lap_block(
+            h["high"][:1], p[first - 1 :], h["high"][1:], h["corner_high"], h["layer_high"], r
+        )
+        side_rim = lap_side(
+            h["side"][0], near(p), h["side"][1], h["corner_low"], h["corner_high"], h["across"]
+        )
+        pair_rim = lap_block(h["pair"], h["layer_low"], h["layer_high"], h["across"], p, 1 - r)
+        return low_rim, high_rim, side_rim, pair_rim
+
+    def rim(h):
+        return h["low"][1:], h["high"][:1], h["side"][0], h["pair"]
+
+    def stepped(p, before, coefficient, lap, lap_before):
+        change = p - before
+        driving = (
+            coefficient * lap + viscous * (lap - lap_before) + 2.0 * nonlinear * change * change
+        )
+        return 2.0 * p - before + (1.0 + 2.0 * nonlinear * p) * driving
+
     steps = STEPS
-    for n in range(steps):
-        change = p_now - p_before
-        driving = (
-            courant * lap
-            + viscous * (lap - lap_before)
-            + 2.0 * nonlinear * change * change
-        )
-        p_next = 2.0 * p_now - p_before + (1.0 + 2.0 * nonlinear * p_now) * driving
-        if n < steps - 1:
-            k = n + 2
-            field[n] = p_next
-            side_out[k] = row(p_next)
-            send(k)
-        else:
-            final_ref[...] = p_next
-            prior_ref[...] = p_now
-        chosen = dot(
-            p_next.reshape(first * second, third).astype(jnp.bfloat16), at_lane, (1, 0)
-        )
+
+    def record(n, p):
+        chosen = dot(p.reshape(first * second, third).astype(jnp.bfloat16), at_lane, (1, 0))
         picked = jnp.sum(chosen * at_row, axis=0, keepdims=True)
         for i in range(tiles):
             loads_out[i, n : n + 1, :] = picked[:, i * LANES : (i + 1) * LANES]
-        if n < steps - 1:
-            lap_before = lap
-            part = inner(p_next)
-            receive(k)
-            lap = outer(part, k)
-            p_before, p_now = p_now, p_next
+
+    coef_rim = None
+    lap_before = None
+    for n in range(0, steps, 2):
+        ks = (n, n + 1)
+        receive(ks + ((4,) if n == 0 else ()))
+        now, old = arrived(n), arrived(n + 1)
+        if n == 0:
+            coef_rim = (low[4][1:], high[4][:1], side_in[4][0], pair_in[4])
+            lap_before = lap_own(p_before, old)
+        lap = lap_own(p_now, now)
+        p_next = stepped(p_now, p_before, courant, lap, lap_before)
+        if n + 2 < steps:
+            field[1] = p_next
+            stage(n + 3, p_next)
+            send((n + 3,))
+        rims = [
+            stepped(*parts)
+            for parts in zip(rim(now), rim(old), coef_rim, lap_rim(p_now, now), lap_rim(p_before, old))
+        ]
+        low_next = jnp.where(has_below, rims[0], 0.0)
+        high_next = jnp.where(has_above, rims[1], 0.0)
+        lap_next = lap_block(p_next, low_next, high_next, rims[2], rims[3], r)
+        p_after = stepped(p_next, p_now, courant, lap_next, lap)
+        if n + 2 < steps:
+            field[0] = p_after
+            stage(n + 2, p_after)
+            send((n + 2,))
+        else:
+            final_ref[...] = p_after
+            prior_ref[...] = p_next
+        record(n, p_next)
+        record(n + 1, p_after)
+        p_before, p_now, lap_before = p_next, p_after, lap_next
 
     def tile_copy(source, target, sems, i):
         to = lax.rem(t + i, tiles)
@@ -566,8 +628,7 @@
     for copy in back_copies[::-1]:
         copy.start()
     back_in[t] = back_out[t]
-    for k in range(steps + 1):
-        sent(k)
+    sent((0, 1, 4, 2, 3))
     for copy in loads_copies + force_copies + accel_copies:
         copy.wait_send()
     for copy in back_copies:
@@ -637,12 +698,16 @@
             pltpu.VMEM((1, slots), jnp.int32),
             pltpu.VMEM((1, 1, 1), jnp.int32),
             pltpu.VMEM((tiles * LANES, modes), mode_shapes.dtype),
-            pltpu.VMEM((STEPS - 1, first, second, third), f32),
+            pltpu.VMEM((2, first, second, third), f32),
+            pltpu.VMEM((levels, 2, first, third), f32),
+            pltpu.VMEM((levels, 2, 1, third), f32),
+            pltpu.VMEM((levels, 2, second, third), f32),
+            pltpu.VMEM((levels, 2, second, third), f32),
+            pltpu.VMEM((levels, 2, first, third), f32),
+            pltpu.VMEM((levels, first, second, third), f32),
+            pltpu.VMEM((levels, 2, 1, third), f32),
+            pltpu.VMEM((levels, 2, second, third), f32),
             pltpu.VMEM((levels, first, third), f32),
-            pltpu.VMEM((levels, second, third), f32),
-            pltpu.VMEM((levels, second, third), f32),
-            pltpu.VMEM((levels, first, third), f32),
-            pltpu.VMEM((levels, first, second, third), f32),
             pltpu.VMEM((tiles, STEPS, LANES), f32),
             pltpu.VMEM((tiles, STEPS, LANES), f32),
             pltpu.VMEM((8, tiles * LANES), f32),
@@ -653,8 +718,8 @@
             pltpu.VMEM((tiles, STEPS, LANES), f32),
             pltpu.VMEM((tiles, STEPS, LANES), f32),
             dma((tiles,)),
-            dma((levels, 4)),
-            dma((levels, 4)),
+            dma((levels, 9)),
+            dma((levels, 9)),
             dma((tiles,)),
             dma((tiles,)),
             dma((devices,)),
@@ -713,7 +778,7 @@
         and tiles > 1
         and pressure.shape[2] == LANES
         and pressure.shape[1] % 8 == 0
-        and pressure.shape[0] > 1
+        and pressure.shape[0] % 8 == 0
         and max(pressure.shape[0] * pressure.shape[1], LANES) <= 256
         and bucket <= LANES
         and bucket % 16 == 0

time: 37.1 us -> 34.3 us (0.925)
  Pallas kernels: 35.7 us -> 32.9 us
    pallas_call x1, Pallas kernels: 35 us -> 32.2 us  [fused_body(): pl.pallas_call(functools.partial(window_kernel, tiles), out_shape=tuple((...]
where the time goes in v3:
time: 34.3 us; the launch traced here: 34.2 us
  Pallas kernels  32.9 us (96%)
  between operations  1.29 us (4%)
    pallas_call x1, Pallas kernels, fused_body(): pl.pallas_call(functools.partial(window_kernel, tiles), out_shape=tuple((...  32.2 us
    pallas_call x1, Pallas kernels, fused_body(): pl.pallas_call(place_kernel, out_shape=shapes, in_specs=[vmem] * 4, out_s...  0.69 us

profile of v3, /device:TPU:0, one launch (start us, length us, event | category | flops | bytes accessed | tf_op | source)
XLA Modules:
  0.0 34.2 jit_solution(12107415070767334515)
XLA Ops:
  1.3 32.2 %window.1 = (f32[8,16,128]{2,1,0:T(8,128)S(1)}, f32[8,16,128]{2,1,0:T(8,128)S(1)}, bf16[4,384]{1,0:T(4,128)(2,1)S(1)}, f32[2,128]{1,0:T(2,128)S(1)}) custom-call(f32[8,16,128]{2,1,0:T(8,128)} %pressure_hbm.1, f32[8,16,128]{2,1,0:T(8,128)} %previous_hbm.1, f32[8,16,128]{2,1,0:T(8,128)} %courant_hbm.1, f32[384]{0:T(512)} %area_hbm.1, ...), custom_call_target="tpu_custom_call" | custom-call | tf_op jit(solution)/shard_map/window/pallas_call | solution.py:684
  33.5 0.7 %placed.1 = (f32[8,16,128]{2,1,0:T(8,128)}, f32[8,16,128]{2,1,0:T(8,128)}, bf16[4,384]{1,0:T(4,128)(2,1)}, f32[2,128]{1,0:T(2,128)}) custom-call(f32[8,16,128]{2,1,0:T(8,128)S(1)} %get-tuple-element.12.refs_0_, f32[8,16,128]{2,1,0:T(8,128)S(1)} %get-tuple-element.13.refs_1_, bf16[4,384]{1,0:T(4,128)(2,1)S(1)} %get-tuple-element.14.refs_2_, ...), custom_call_target="tpu_custom_call" | custom-call | tf_op jit(solution)/shard_map/placed/pallas_call | solution.py:748

commit v4 on v3

--- a/solution.py
+++ b/solution.py
@@ -276,8 +276,24 @@
         return (where[0] * 2 + where[1]) * 2 + where[2]
 
     barrier = pltpu.get_barrier_semaphore()
-    for offset in partners:
-        pl.semaphore_signal(barrier, inc=1, device_id=ident(place(offset)), device_id_type=MESH)
+    up = {"tile": jnp.minimum(t + 1, tiles - 1)}
+    down = {"tile": jnp.maximum(t - 1, 0)}
+    beside_me, pair = {"sub": 1 - s}, {"rep": 1 - r}
+    in_tile = ({}, beside_me, pair, beside_me | pair)
+
+    def greet(devices):
+        for where in devices:
+            pl.semaphore_signal(barrier, inc=1, device_id=where, device_id_type=MESH)
+
+    @pl.when(t < tiles - 1)
+    def _():
+        greet([up | where for where in in_tile])
+
+    @pl.when(t > 0)
+    def _():
+        greet([down | where for where in in_tile])
+
+    greet(in_tile[1:])
 
     mode_copies = [
         pltpu.make_async_copy(
@@ -341,10 +357,6 @@
             device_id=where,
             device_id_type=MESH,
         )
-
-    up = {"tile": jnp.minimum(t + 1, tiles - 1)}
-    down = {"tile": jnp.maximum(t - 1, 0)}
-    beside_me, pair = {"sub": 1 - s}, {"rep": 1 - r}
 
     def piece(k, m):
         source, target, where = (
@@ -390,7 +402,8 @@
     def sent(ks):
         each(ks, True, lambda copy: copy.wait_send())
 
-    pl.semaphore_wait(barrier, len(partners))
+    greeted = 4 * (jnp.minimum(t, 1) + jnp.minimum(tiles - 1 - t, 1)) + 3
+    pl.semaphore_wait(barrier, greeted)
     send((0, 1, 4))
 
     for i in range(tiles):
@@ -775,7 +788,7 @@
     fits = (
         subs == 2
         and reps == 2
-        and tiles > 1
+        and 1 < tiles <= 4
         and pressure.shape[2] == LANES
         and pressure.shape[1] % 8 == 0
         and pressure.shape[0] % 8 == 0

time: 34.3 us -> 33.4 us (0.974)
  Pallas kernels: 32.9 us -> 32 us
    pallas_call x1, Pallas kernels: 32.2 us -> 31.3 us  [fused_body(): pl.pallas_call(functools.partial(window_kernel, tiles), out_shape=tuple((...]
where the time goes in v4:
time: 33.4 us; the launch traced here: 33.3 us
  Pallas kernels  32 us (96%)
  between operations  1.29 us (4%)
    pallas_call x1, Pallas kernels, fused_body(): pl.pallas_call(functools.partial(window_kernel, tiles), out_shape=tuple((...  31.3 us
    pallas_call x1, Pallas kernels, fused_body(): pl.pallas_call(place_kernel, out_shape=shapes, in_specs=[vmem] * 4, out_s...  0.69 us

profile of v4, /device:TPU:0, one launch (start us, length us, event | category | flops | bytes accessed | tf_op | source)
XLA Modules:
  0.0 33.3 jit_solution(96027927130314155)
XLA Ops:
  1.3 31.3 %window.1 = (f32[8,16,128]{2,1,0:T(8,128)S(1)}, f32[8,16,128]{2,1,0:T(8,128)S(1)}, bf16[4,384]{1,0:T(4,128)(2,1)S(1)}, f32[2,128]{1,0:T(2,128)S(1)}) custom-call(f32[8,16,128]{2,1,0:T(8,128)} %pressure_hbm.1, f32[8,16,128]{2,1,0:T(8,128)} %previous_hbm.1, f32[8,16,128]{2,1,0:T(8,128)} %courant_hbm.1, f32[384]{0:T(512)} %area_hbm.1, ...), custom_call_target="tpu_custom_call" | custom-call | tf_op jit(solution)/shard_map/window/pallas_call | solution.py:697
  32.6 0.7 %placed.1 = (f32[8,16,128]{2,1,0:T(8,128)}, f32[8,16,128]{2,1,0:T(8,128)}, bf16[4,384]{1,0:T(4,128)(2,1)}, f32[2,128]{1,0:T(2,128)}) custom-call(f32[8,16,128]{2,1,0:T(8,128)S(1)} %get-tuple-element.12.refs_0_, f32[8,16,128]{2,1,0:T(8,128)S(1)} %get-tuple-element.13.refs_1_, bf16[4,384]{1,0:T(4,128)(2,1)S(1)} %get-tuple-element.14.refs_2_, ...), custom_call_target="tpu_custom_call" | custom-call | tf_op jit(solution)/shard_map/placed/pallas_call | solution.py:761
